TPU v7x, 128 devices: a whole 4x4x4 slice. The times are simulated.
128 devices in a mesh: dp: 16 (over x, z), expert: 8 (over y, core).
Axes of the slice: x: 4, y: 4, z: 4, core: 2. Of those that a mesh axis runs over, the one named last changes fastest.
Arguments:
- tokens: float32 [8192, 1664], P('dp'), may hold values from -6 to 6
- ln_gain: float32 [1664], replicated, may hold values from 0.1 to 1.9
- ln_bias: float32 [1664], replicated, may hold values from -3 to 3
- weight_in: bfloat16 [32, 1664, 8192], P('dp', None, 'expert'), may hold values from -0.15625 to 0.15625
- weight_out: bfloat16 [32, 8192, 1664], P('dp', 'expert'), may hold values from -0.0625 to 0.0625
- expert_ids: int32 [8192, 2], P('dp'), may hold values from 0 to 31, all different within a row; in each aligned block of 512 rows (0 to 511, 512 to 1023, ...) at most 80 rows name the same one
- combine_weights: float32 [8192, 2], P('dp'), may hold values from 0.2 to 1
- owner_ids: int32 [32, 1], replicated, may hold values from 0 to 15; in each aligned block of 32 rows (0 to 31, 32 to 63, ...) at most 4 rows name the same one
Outputs:
- delivered: float32 [16384, 1664], P('dp', 'expert')
Inputs may be any that keep to these rules, and one draw needn't show every extreme that they name: `expert_ids`: the two entries of a row differ. In each aligned block of 512 rows no expert is named more than 80 times. `owner_ids`: no owner is named more than 4 times.
All inputs are finite; a program needn't handle non-finite values.
Results may differ from a plain program's by a relative error of at most 0.008.
Values may be sent and summed in bfloat16 or wider, within the bound.
A program may use at most 128 MiB of HBM per device.

v0:
```python
import jax
import jax.numpy as jnp
from jax import lax
from jax.experimental import pallas as pl
from jax.experimental.pallas import tpu as pltpu
from jax.sharding import PartitionSpec as P

MESH = pl.DeviceIdType.MESH
F32 = jnp.float32
BF16 = jnp.bfloat16

PATCH = 256
CAP = 80
OWN_IMG = 4
SIDE = 4
epsilon = 1e-06

COMMON = (0, 1)
EVEN = ((2, 2), (1, 3), (3, 1), (2, 1), (3, 2), (0, 3), (1, 0))
ODD = ((1, 1), (3, 3), (0, 2), (2, 3), (1, 2), (2, 0), (3, 0))
OWNED = 7
FIRST = 3
OWN_SLOT = (2, 3, 4, 8, 9, 10, 11)
GUEST_SLOT = (5, 6, 7, 12, 13, 14, 15)
HALF = 8 * CAP


def column_tiles(width, step, body):
    count = width // step

    def one(n, carry):
        body(pl.ds(pl.multiple_of(n * step, 128), step))
        return carry

    lax.fori_loop(0, count, one, 0)
    if count * step < width:
        body(pl.ds(count * step, width - count * step))


def block(index):
    return pl.ds(index * CAP, CAP)


def kernel(
    img,
    tokens,
    gain,
    bias,
    ids_t,
    weights_t,
    base,
    weight_in,
    weight_out,
    delivered,
    normed,
    rank,
    pick,
    gathered,
    x_in,
    w_in,
    w_out,
    hidden,
    out,
    partner,
    ret,
    partial,
    split,
    pair,
    summed,
    others,
    stage_a,
    message,
    stage_b,
    local_sem,
    wx_send,
    wx_recv,
    go_send,
    go_recv,
    fw_send,
    fw_recv,
    pr_send,
    pr_recv,
    rt_send,
    rt_recv,
    rs_send,
    rs_recv,
    da_send,
    da_recv,
    db_send,
    db_recv,
):
    dp = lax.axis_index("dp")
    ex = lax.axis_index("expert")
    x, z = dp // SIDE, dp % SIDE
    y, core = ex // 2, ex % 2
    parity = y % 2
    tok_rows, width = tokens.shape
    local_hidden = weight_in.shape[2]
    share = delivered.shape[1]

    def at_xz(dx, dz):
        return ((x + dx + SIDE) % SIDE) * SIDE + (z + dz + SIDE) % SIDE

    def at_y(dy):
        return ((y + dy + SIDE) % SIDE) * 2 + core

    def owned(j):
        (ax, az), (bx, bz) = EVEN[j], ODD[j]
        return ax + parity * (bx - ax), az + parity * (bz - az)

    def remote(src, dst, send, recv, device):
        return pltpu.make_async_remote_copy(
            src_ref=src,
            dst_ref=dst,
            send_sem=send,
            recv_sem=recv,
            device_id=device,
            device_id_type=MESH,
        )

    barrier = pltpu.get_barrier_semaphore()
    peers = [(at_xz(dx, dz), ex) for dx in range(SIDE) for dz in range(SIDE) if dx or dz]
    peers += [(dp, at_y(dy)) for dy in range(1, SIDE)]
    peers += [(dp, y * 2 + 1 - core)]
    for peer in peers:
        pl.semaphore_signal(barrier, inc=1, device_id=peer, device_id_type=MESH)

    own_in = pltpu.make_async_copy(
        weight_in.at[core], w_in.at[:, pl.ds(0, local_hidden)], local_sem.at[0]
    )
    own_out = pltpu.make_async_copy(
        weight_out.at[core], w_out.at[pl.ds(0, local_hidden), :], local_sem.at[1]
    )
    own_in.start()
    own_out.start()

    def norm_rows(r, carry):
        rows = pl.ds(pl.multiple_of(r * 64, 64), 64)
        value = tokens[rows, :]
        center = value - jnp.mean(value, axis=1, keepdims=True)
        spread = jnp.mean(center * center, axis=1, keepdims=True)
        value = center * lax.rsqrt(spread + epsilon) * gain[...] + bias[...]
        normed[rows, :] = value.astype(BF16)
        return carry

    lax.fori_loop(0, tok_rows // 64, norm_rows, 0)

    experts = rank.shape[0]
    wanted = lax.broadcasted_iota(jnp.int32, (experts, tok_rows), 0)
    named = (ids_t[0:1, :] == wanted) | (ids_t[1:2, :] == wanted)
    earlier = (
        lax.broadcasted_iota(jnp.int32, (tok_rows, tok_rows), 0)
        < lax.broadcasted_iota(jnp.int32, (tok_rows, tok_rows), 1)
    ).astype(F32).astype(BF16)
    before = jnp.dot(named.astype(F32).astype(BF16), earlier, preferred_element_type=F32)
    rank[...] = jnp.where(named, before, 200.0)

    displacements = [(0, 0), COMMON] + [owned(j) for j in range(OWNED)]
    place = lax.broadcasted_iota(jnp.int32, (CAP, tok_rows), 0).astype(F32)

    def expert_of(i):
        return 2 * at_xz(*displacements[i]) + core

    def hit_rows(i):
        return rank[pl.ds(expert_of(i), 1), :] == place

    for i in range(2 + OWNED):
        pick[block(i), :] = hit_rows(i).astype(F32).astype(BF16)

    pl.semaphore_wait(barrier, len(peers))

    other_core = (dp, y * 2 + 1 - core)
    swap_in = remote(
        weight_in.at[1 - core],
        w_in.at[:, pl.ds(local_hidden, local_hidden)],
        wx_send.at[0],
        wx_recv.at[0],
        other_core,
    )
    swap_out = remote(
        weight_out.at[1 - core],
        w_out.at[pl.ds(local_hidden, local_hidden), :],
        wx_send.at[1],
        wx_recv.at[1],
        other_core,
    )
    swap_in.start()
    swap_out.start()

    sends = []
    for i in range(1, 2 + OWNED):
        j = i - 2
        slot = 1 if i == 1 else OWN_SLOT[j]
        sends.append(
            remote(
                gathered.at[block(i - 1), :],
                x_in.at[block(slot), :],
                go_send.at[i - 1],
                go_recv.at[i - 1],
                (at_xz(*displacements[i]), ex),
            )
        )

    def gather(start, stop):
        rows = pl.ds(start * CAP, (stop - start) * CAP)
        to = pl.ds((start - 1) * CAP, (stop - start) * CAP)

        def one(cols):
            gathered[to, cols] = jnp.dot(
                pick[rows, :], normed[:, cols], preferred_element_type=F32
            ).astype(BF16)

        column_tiles(width, 256, one)

    gather(1, 2 + FIRST)
    for i in range(1, 2 + FIRST):
        sends[i - 1].start()
    gather(2 + FIRST, 2 + OWNED)
    for i in range(2 + FIRST, 2 + OWNED):
        sends[i - 1].start()

    def own_block(cols):
        x_in[block(0), cols] = jnp.dot(
            pick[block(0), :], normed[:, cols], preferred_element_type=F32
        ).astype(BF16)

    column_tiles(width, 256, own_block)

    for i in range(2 + OWNED):
        chosen = jnp.where(ids_t[0:1, :] == expert_of(i), weights_t[0:1, :], weights_t[1:2, :])
        pick[block(i), :] = jnp.where(hit_rows(i), chosen, 0.0).astype(BF16)

    forwards = []
    for j in range(OWNED):
        sign = 1 if j % 2 == 0 else -1
        forwards.append(
            remote(
                x_in.at[block(OWN_SLOT[j]), :],
                x_in.at[block(GUEST_SLOT[j]), :],
                fw_send.at[j],
                fw_recv.at[j],
                (dp, at_y(sign)),
            )
        )

    def forward(j):
        sends[j + 1].wait_recv()
        forwards[j].start()

    for j in range(FIRST):
        forward(j)

    def first_matmul(half):
        rows = pl.ds(half * HALF, HALF)

        def one(cols):
            pre = jnp.dot(x_in[rows, :], w_in[:, cols], preferred_element_type=F32)
            hidden[:, cols] = jax.nn.gelu(pre, approximate=True).astype(BF16)

        column_tiles(2 * local_hidden, 256, one)

    def second_matmul(half):
        rows = pl.ds(half * HALF, HALF)

        def one(cols):
            out[rows, cols] = jnp.dot(
                hidden[...], w_out[:, cols], preferred_element_type=F32
            ).astype(BF16)

        column_tiles(width, 256, one)

    to_owner, back = [], []
    for j in range(OWNED):
        sign = 1 if j % 2 == 0 else -1
        to_owner.append(
            remote(
                out.at[block(GUEST_SLOT[j]), :],
                partner.at[block(j), :],
                pr_send.at[j],
                pr_recv.at[j],
                (dp, at_y(-sign)),
            )
        )
        dx, dz = owned(j)
        back.append(
            remote(
                out.at[block(OWN_SLOT[j]), :],
                ret.at[block(2 + j), :],
                rt_send.at[j],
                rt_recv.at[j],
                (at_xz(-dx, -dz), ex),
            )
        )
    back_common = remote(
        out.at[block(1), :],
        ret.at[block(1), :],
        rt_send.at[OWNED],
        rt_recv.at[OWNED],
        (at_xz(-COMMON[0], -COMMON[1]), ex),
    )

    def add_and_send(j):
        to_owner[j].wait_recv()

        def one(cols):
            mine = out[block(OWN_SLOT[j]), cols].astype(F32)
            out[block(OWN_SLOT[j]), cols] = (
                mine + partner[block(j), cols].astype(F32)
            ).astype(BF16)

        column_tiles(width, 832 // 128 * 128, one)
        back[j].start()

    sends[0].wait_recv()
    for j in range(FIRST):
        forwards[j].wait_recv()
    own_in.wait()
    own_out.wait()
    swap_in.wait_recv()
    swap_out.wait_recv()
    first_matmul(0)
    for j in range(FIRST, OWNED):
        forward(j)
    second_matmul(0)
    back_common.start()
    for j in range(FIRST):
        to_owner[j].start()

    for j in range(FIRST, OWNED):
        forwards[j].wait_recv()
    first_matmul(1)
    for j in range(FIRST):
        add_and_send(j)
    ret[block(0), :] = out[block(0), :]
    second_matmul(1)
    for j in range(FIRST, OWNED):
        to_owner[j].start()
    for j in range(FIRST, OWNED):
        add_and_send(j)

    back_common.wait_recv()
    for j in range(OWNED):
        back[j].wait_recv()
    partial[:, pl.ds(width, 128)] = jnp.zeros((tok_rows, 128), F32)

    def combine(cols):
        partial[:, cols] = lax.dot_general(
            pick[...],
            ret[:, cols],
            (((0,), (0,)), ((), ())),
            preferred_element_type=F32,
        )

    column_tiles(width, 256, combine)

    columns = 2 * SIDE

    def cut(r, carry):
        rows = pl.ds(pl.multiple_of(r * 64, 64), 64)
        for c in range(columns):
            split[c % 2, c // 2, rows, :] = partial[rows, c * share : c * share + 256].astype(BF16)
        return carry

    lax.fori_loop(0, tok_rows // 64, cut, 0)
    to_pair = remote(split.at[1 - core], pair, rs_send.at[0], rs_recv.at[0], other_core)
    to_pair.start()
    to_pair.wait_recv()

    def add_pair(r, carry):
        rows = pl.ds(pl.multiple_of(r * 64, 64), 64)
        for c in range(SIDE):
            summed[c, rows, :] = (
                split[core, c, rows, :].astype(F32) + pair[c, rows, :].astype(F32)
            ).astype(BF16)
        return carry

    lax.fori_loop(0, tok_rows // 64, add_pair, 0)
    over_y = []
    for r in range(1, SIDE):
        over_y.append(
            remote(
                summed.at[(y + r) % SIDE],
                others.at[r - 1],
                rs_send.at[r],
                rs_recv.at[r],
                (dp, at_y(r)),
            )
        )
        over_y[-1].start()
    for copy in over_y:
        copy.wait_recv()
    tail = share - 128
    for i in range(tok_rows // PATCH):
        for r in range(PATCH // 64):
            rows = pl.ds(i * PATCH + r * 64, 64)
            total = summed[y, rows, :].astype(F32)
            for k in range(SIDE - 1):
                total = total + others[k, rows, :].astype(F32)
            to = pl.ds(r * 64, 64)
            stage_a[0, i, to, :] = (total[:, :128] + base[rows, 0:128]).astype(BF16)
            stage_a[1, i, to, 0:tail] = (
                total[:, 128:share] + base[rows, 128:share]
            ).astype(BF16)

    imgs = tok_rows // PATCH

    def along(h, first, step):
        if (h == 0) == first:
            return (at_xz(step, 0), ex)
        return (at_xz(0, step), ex)

    gathers = []
    for h in range(2):
        for r in range(1, SIDE):
            k = h * 3 + r - 1
            gathers.append(
                remote(
                    stage_a.at[h, pl.ds(0, imgs)],
                    stage_a.at[h, pl.ds(imgs * r, imgs)],
                    da_send.at[k],
                    da_recv.at[k],
                    along(h, True, r),
                )
            )
            gathers[-1].start()
    for copy in gathers:
        copy.wait_recv()

    def source_of(owner, j):
        index = img[owner * OWN_IMG + j]
        held = jnp.maximum(index, 0)
        device = held // imgs
        return index, device // SIDE, device % SIDE, held % imgs

    delivers = []
    for q in (1, 3, 2, 0):
        for h in range(2):
            owner = along(h, False, q)[0]
            for j in range(OWN_IMG):
                _, from_x, from_z, which = source_of(owner, j)
                r = (x - from_x + SIDE) % SIDE if h == 0 else (z - from_z + SIDE) % SIDE
                value = stage_a[h, r * imgs + which]
                if q == 0:
                    stage_b[h, j] = value
                else:
                    message[h, q - 1, j] = value
            if q:
                k = h * 3 + q - 1
                delivers.append(
                    remote(
                        message.at[h, q - 1],
                        stage_b.at[h, pl.ds(OWN_IMG * q, OWN_IMG)],
                        db_send.at[k],
                        db_recv.at[k],
                        along(h, False, q),
                    )
                )
                delivers[-1].start()
    for copy in delivers:
        copy.wait_recv()
    for j in range(OWN_IMG):
        index, from_x, from_z, _ = source_of(dp, j)
        there = index >= 0
        rows = pl.ds(j * PATCH, PATCH)
        first = stage_b[0, (z - from_z + SIDE) % SIDE * OWN_IMG + j].astype(F32)
        delivered[rows, 0:128] = jnp.where(there, first, 0.0)
        second = stage_b[1, (x - from_x + SIDE) % SIDE * OWN_IMG + j].astype(F32)
        delivered[rows, 128:share] = jnp.where(there, second, 0.0)[:, :tail]

    for copy in (
        [swap_in, swap_out]
        + sends
        + forwards
        + to_owner
        + back
        + [back_common, to_pair]
        + over_y
        + gathers
        + delivers
    ):
        copy.wait_send()


def shards(tokens, ln_gain, ln_bias, weight_in, weight_out, expert_ids, combine_weights, owner_ids):
    groups = lax.axis_size("dp")
    columns = lax.axis_size("expert")
    tok_rows, width = tokens.shape
    share = width // columns
    hidden = 2 * weight_in.shape[2]
    experts = weight_in.shape[0] * groups

    owners = owner_ids[:, 0]
    images = owners.shape[0]
    order = jnp.arange(images, dtype=jnp.int32)
    same = (owners[:, None] == owners[None, :]) & (order[None, :] < order[:, None])
    place = owners * OWN_IMG + jnp.sum(same.astype(jnp.int32), axis=1)
    slots = jnp.arange(groups * OWN_IMG, dtype=jnp.int32)
    img = jnp.max(
        jnp.where(place[None, :] == slots[:, None], order[None, :], -1), axis=1
    ).astype(jnp.int32)
    base = lax.dynamic_slice_in_dim(tokens, lax.axis_index("expert") * share, share, axis=1)

    def vmem(shape, dtype=BF16):
        return pltpu.VMEM(shape, dtype)

    def sems(count):
        return pltpu.SemaphoreType.DMA((count,))

    whole = pl.BlockSpec(memory_space=pltpu.VMEM)
    scratch = [
        vmem((tok_rows, width)),
        vmem((experts, tok_rows), F32),
        vmem((9 * CAP, tok_rows)),
        vmem((8 * CAP, width)),
        vmem((16 * CAP, width)),
        vmem((width, hidden)),
        vmem((hidden, width)),
        vmem((HALF, hidden)),
        vmem((16 * CAP, width)),
        vmem((OWNED * CAP, width)),
        vmem((9 * CAP, width)),
        vmem((tok_rows, width + 128), F32),
        vmem((2, SIDE, tok_rows, 256)),
        vmem((SIDE, tok_rows, 256)),
        vmem((SIDE, tok_rows, 256)),
        vmem((SIDE - 1, tok_rows, 256)),
        vmem((2, 8, PATCH, 128)),
        vmem((2, SIDE - 1, OWN_IMG, PATCH, 128)),
        vmem((2, SIDE * OWN_IMG, PATCH, 128)),
    ]
    for count in (2, 2, 2, 8, 8, 7, 7, 7, 7, 8, 8, 4, 4, 6, 6, 6, 6):
        scratch.append(sems(count))
    return pl.pallas_call(
        kernel,
        out_shape=jax.ShapeDtypeStruct((OWN_IMG * PATCH, share), F32),
        in_specs=[pl.BlockSpec(memory_space=pltpu.SMEM)]
        + [whole] * 6
        + [pl.BlockSpec(memory_space=pl.ANY)] * 2,
        out_specs=whole,
        scratch_shapes=scratch,
        compiler_params=pltpu.CompilerParams(
            collective_id=0, has_side_effects=True, vmem_limit_bytes=67043328
        ),
    )(
        img,
        tokens,
        ln_gain.reshape(1, width),
        ln_bias.reshape(1, width),
        expert_ids.T,
        combine_weights.T,
        base,
        weight_in,
        weight_out,
    )


def solution(mesh):
    return jax.shard_map(
        shards,
        mesh=mesh,
        in_specs=(
            P("dp", None),
            P(),
            P(),
            P("dp", None, "expert"),
            P("dp", "expert", None),
            P("dp", None),
            P("dp", None),
            P(),
        ),
        out_specs=P("dp", "expert"),
        check_vma=False,
    )
```

profile of v0, /device:TPU:1, one launch (start us, length us, event | category | flops | bytes accessed | tf_op | source)
XLA Modules:
  0.0 157.5 jit_solution(2112186663196481869)
XLA Ops:
  0.0 0.9 convert_reduce_fusion
  0.9 0.7 multiply_add_fusion
  1.6 0.6 select_reduce_fusion.img
  2.2 1.3 reshape.15.gain
  3.5 1.3 reshape.16.bias
  4.8 2.1 %constant_dynamic-slice_fusion.base = f32[512,208]{1,0:T(8,128)} fusion(f32[512,1664]{1,0:T(8,128)} %tokens.1, s32[]{:T(128)S(6)} %select_n.8), kind=kLoop, calls=%fused_computation.6 | loop fusion | bytes 851972 | tf_op jit(solution)/shard_map/dynamic_slice | solution.py:501
  6.9 148.1 %shard_map.82 = f32[1024,208]{1,0:T(8,128)} custom-call(s32[64]{0:T(128)} %select_reduce_fusion.img, f32[512,1664]{1,0:T(8,128)} %tokens.1, f32[1,1664]{1,0:T(1,128)} %reshape.15.gain, f32[1,1664]{1,0:T(1,128)} %reshape.16.bias, s32[2,512]{1,0:T(2,128)} %bitcast.4, f32[2,512]{1,0:T(2,128)} %bitcast.5, f32[512,208]{1,0:T(8,128)} %constant_dynamic-slice_fusion.base, ...), custom_call_target="tpu_custom_call" | custom-call | tf_op jit(solution)/shard_map/pallas_call | solution.py:533
  155.0 2.4 %copy.10 = f32[1024,208]{0,1:T(8,128)} copy(f32[1024,208]{1,0:T(8,128)} %shard_map.82) | data formatting | bytes 1703936 | tf_op jit(solution)/shard_map/pallas_call | solution.py:533
where the time goes:
time: 158 us; the launch traced here: 157 us
  Pallas kernels  148 us (94%)
  local copies, waits for them, and re-layouts  7.17 us (5%)
  other arithmetic  2.2 us (1%)
    pallas_call x1, Pallas kernels, shards(): pl.pallas_call(kernel, out_shape=jax.ShapeDtypeStruct((OWN_IMG * PATCH, s...  148 us

commit v1 on v0

v1 whole, which is shorter than its diff:
```python
import jax
import jax.numpy as jnp
from jax import lax
from jax.experimental import pallas as pl
from jax.experimental.pallas import tpu as pltpu
from jax.sharding import PartitionSpec as P

MESH = pl.DeviceIdType.MESH
F32 = jnp.float32
BF16 = jnp.bfloat16

PATCH = 256
CAP = 80
OWN_IMG = 4
SIDE = 4
epsilon = 1e-06

COMMON = (0, 1)
EVEN = ((2, 2), (1, 3), (3, 1), (2, 1), (3, 2), (0, 3), (1, 0))
ODD = ((1, 1), (3, 3), (0, 2), (2, 3), (1, 2), (2, 0), (3, 0))
OWNED = 7
OWN_SLOT = (2, 4, 5, 8, 9, 12, 13)
GUEST_SLOT = (3, 6, 7, 10, 11, 14, 15)
IN_CHUNK = ((0,), (1, 2), (3, 4), (5, 6))
CHUNK = 4 * CAP
EARLY = 7 * CAP


def column_tiles(width, step, body):
    count = width // step

    def one(n, carry):
        body(pl.ds(pl.multiple_of(n * step, 128), step))
        return carry

    lax.fori_loop(0, count, one, 0)
    if count * step < width:
        body(pl.ds(count * step, width - count * step))


def block(index):
    return pl.ds(index * CAP, CAP)


def kernel(
    owners,
    tokens,
    gain,
    bias,
    ids_t,
    weights_t,
    weight_in,
    weight_out,
    delivered,
    img,
    base,
    normed,
    rank,
    pick,
    gathered,
    x_in,
    w_in,
    w_out,
    hidden,
    out,
    partner,
    ret,
    partial,
    split,
    pair,
    summed,
    others,
    stage_a0,
    stage_a1,
    message,
    stage_b0,
    stage_b1,
    local_sem,
    wx_send,
    wx_recv,
    go_send,
    go_recv,
    fw_send,
    fw_recv,
    pr_send,
    pr_recv,
    rt_send,
    rt_recv,
    rs_send,
    rs_recv,
    da_send,
    da_recv,
    db_send,
    db_recv,
):
    stage_a, stage_b = (stage_a0, stage_a1), (stage_b0, stage_b1)
    dp = lax.axis_index("dp")
    ex = lax.axis_index("expert")
    x, z = dp // SIDE, dp % SIDE
    y, core = ex // 2, ex % 2
    parity = y % 2
    tok_rows, width = tokens.shape
    local_hidden = weight_in.shape[2]
    share = delivered.shape[1]

    def at_xz(dx, dz):
        return ((x + dx + SIDE) % SIDE) * SIDE + (z + dz + SIDE) % SIDE

    def at_y(dy):
        return ((y + dy + SIDE) % SIDE) * 2 + core

    def owned(j):
        (ax, az), (bx, bz) = EVEN[j], ODD[j]
        return ax + parity * (bx - ax), az + parity * (bz - az)

    def remote(src, dst, send, recv, device):
        return pltpu.make_async_remote_copy(
            src_ref=src,
            dst_ref=dst,
            send_sem=send,
            recv_sem=recv,
            device_id=device,
            device_id_type=MESH,
        )

    started, heard = [], []

    def go(copy):
        copy.start()
        started.append(copy)

    def hear(copy):
        copy.wait_recv()
        heard.append(copy)

    def finish():
        for copy in started:
            copy.wait_send()


    barrier = pltpu.get_barrier_semaphore()
    peers = [(at_xz(dx, dz), ex) for dx in range(SIDE) for dz in range(SIDE) if dx or dz]
    peers += [(dp, at_y(dy)) for dy in range(1, SIDE)]
    peers += [(dp, y * 2 + 1 - core)]
    for peer in peers:
        pl.semaphore_signal(barrier, inc=1, device_id=peer, device_id_type=MESH)

    own_in = pltpu.make_async_copy(
        weight_in.at[core], w_in.at[:, pl.ds(0, local_hidden)], local_sem.at[0]
    )
    own_out = pltpu.make_async_copy(
        weight_out.at[core], w_out.at[pl.ds(0, local_hidden), :], local_sem.at[1]
    )
    own_in.start()
    own_out.start()

    lanes = [pl.ds(c * 128, 128) for c in range(width // 128)]

    def norm_rows(r, carry):
        rows = pl.ds(pl.multiple_of(r * 64, 64), 64)
        total = tokens[rows, lanes[0]]
        for cols in lanes[1:]:
            total = total + tokens[rows, cols]
        mean = jnp.sum(total, axis=1, keepdims=True) / width
        total = jnp.zeros((64, 128), F32)
        for cols in lanes:
            center = tokens[rows, cols] - mean
            total = total + center * center
        scale = lax.rsqrt(jnp.sum(total, axis=1, keepdims=True) / width + epsilon)
        for c, cols in enumerate(lanes):
            value = (tokens[rows, cols] - mean) * scale * gain[c : c + 1, :] + bias[c : c + 1, :]
            normed[rows, cols] = value.astype(BF16)
        return carry

    lax.fori_loop(0, tok_rows // 64, norm_rows, 0, unroll=2)

    experts = rank.shape[0]
    wanted = lax.broadcasted_iota(jnp.int32, (experts, tok_rows), 0)
    named = (ids_t[0:1, :] == wanted) | (ids_t[1:2, :] == wanted)
    earlier = (
        lax.broadcasted_iota(jnp.int32, (tok_rows, tok_rows), 0)
        < lax.broadcasted_iota(jnp.int32, (tok_rows, tok_rows), 1)
    ).astype(F32).astype(BF16)
    before = jnp.dot(named.astype(F32).astype(BF16), earlier, preferred_element_type=F32)
    rank[...] = jnp.where(named, before, 200.0)

    displacements = [(0, 0), COMMON] + [owned(j) for j in range(OWNED)]
    place = lax.broadcasted_iota(jnp.int32, (CAP, tok_rows), 0).astype(F32)

    def expert_of(i):
        return 2 * at_xz(*displacements[i]) + core

    def hit_rows(i):
        return rank[pl.ds(expert_of(i), 1), :] == place

    for i in range(2 + OWNED):
        pick[block(i), :] = hit_rows(i).astype(F32).astype(BF16)

    pl.semaphore_wait(barrier, len(peers))

    other_core = (dp, y * 2 + 1 - core)
    swap_in = remote(
        weight_in.at[1 - core],
        w_in.at[:, pl.ds(local_hidden, local_hidden)],
        wx_send.at[0],
        wx_recv.at[0],
        other_core,
    )
    swap_out = remote(
        weight_out.at[1 - core],
        w_out.at[pl.ds(local_hidden, local_hidden), :],
        wx_send.at[1],
        wx_recv.at[1],
        other_core,
    )
    go(swap_in)
    go(swap_out)

    sends = []
    for i in range(1, 2 + OWNED):
        j = i - 2
        slot = 1 if i == 1 else OWN_SLOT[j]
        sends.append(
            remote(
                gathered.at[block(i - 1), :],
                x_in.at[block(slot), :],
                go_send.at[i - 1],
                go_recv.at[i - 1],
                (at_xz(*displacements[i]), ex),
            )
        )

    def gather(start, stop):
        rows = pl.ds(start * CAP, (stop - start) * CAP)
        to = pl.ds((start - 1) * CAP, (stop - start) * CAP)

        def one(cols):
            gathered[to, cols] = jnp.dot(
                pick[rows, :], normed[:, cols], preferred_element_type=F32
            ).astype(BF16)

        column_tiles(width, 256, one)

    for start, end in ((1, 3), (3, 5), (5, 9)):
        gather(start, end)
        for i in range(start, end):
            go(sends[i - 1])

    def own_block(cols):
        x_in[block(0), cols] = jnp.dot(
            pick[block(0), :], normed[:, cols], preferred_element_type=F32
        ).astype(BF16)

    column_tiles(width, 256, own_block)

    for i in range(2 + OWNED):
        chosen = jnp.where(ids_t[0:1, :] == expert_of(i), weights_t[0:1, :], weights_t[1:2, :])
        pick[block(i), :] = jnp.where(hit_rows(i), chosen, 0.0).astype(BF16)

    forwards = []
    for j in range(OWNED):
        sign = 1 if j % 2 == 0 else -1
        forwards.append(
            remote(
                x_in.at[block(OWN_SLOT[j]), :],
                x_in.at[block(GUEST_SLOT[j]), :],
                fw_send.at[j],
                fw_recv.at[j],
                (dp, at_y(sign)),
            )
        )

    def forward(j):
        hear(sends[j + 1])
        go(forwards[j])

    for j in range(3):
        forward(j)

    for c in range(2 * SIDE):

        @pl.when(ex == c)
        def _():
            def one(r, carry):
                rows = pl.ds(pl.multiple_of(r * 64, 64), 64)
                base[rows, :] = tokens[rows, c * share : (c + 1) * share]
                return carry

            lax.fori_loop(0, tok_rows // 64, one, 0)

    near = [dp] + [at_xz(0, q) for q in range(1, SIDE)] + [at_xz(q, 0) for q in range(1, SIDE)]

    def note(i, carry):
        owner, new = owners[i], []
        for w, candidate in enumerate(near):
            count, held = carry[w][0], carry[w][1:]
            hit = owner == candidate
            held = [jnp.where(hit & (count == k), i, held[k]) for k in range(OWN_IMG)]
            new.append((count + hit.astype(jnp.int32), *held))
        return tuple(new)

    none = jnp.int32(-1)
    noted = lax.fori_loop(
        0, owners.shape[0], note, ((jnp.int32(0),) + (none,) * OWN_IMG,) * len(near)
    )
    for w in range(len(near)):
        for k in range(OWN_IMG):
            img[w * OWN_IMG + k] = noted[w][1 + k]

    def first_matmul(c):
        pre = jnp.dot(x_in[pl.ds(c * CHUNK, CHUNK), :], w_in[...], preferred_element_type=F32)
        hidden[...] = jax.nn.gelu(pre, approximate=True).astype(BF16)

    def second_matmul(c):
        out[pl.ds(c * CHUNK, CHUNK), :] = jnp.dot(
            hidden[...], w_out[...], preferred_element_type=F32
        ).astype(BF16)

    to_owner, back = [], []
    for j in range(OWNED):
        sign = 1 if j % 2 == 0 else -1
        to_owner.append(
            remote(
                out.at[block(GUEST_SLOT[j]), :],
                partner.at[block(j), :],
                pr_send.at[j],
                pr_recv.at[j],
                (dp, at_y(-sign)),
            )
        )
        dx, dz = owned(j)
        back.append(
            remote(
                out.at[block(OWN_SLOT[j]), :],
                ret.at[block(2 + j), :],
                rt_send.at[j],
                rt_recv.at[j],
                (at_xz(-dx, -dz), ex),
            )
        )
    back_common = remote(
        out.at[block(1), :],
        ret.at[block(1), :],
        rt_send.at[OWNED],
        rt_recv.at[OWNED],
        (at_xz(-COMMON[0], -COMMON[1]), ex),
    )

    def add_and_send(j):
        hear(to_owner[j])

        def one(cols):
            mine = out[block(OWN_SLOT[j]), cols].astype(F32)
            out[block(OWN_SLOT[j]), cols] = (
                mine + partner[block(j), cols].astype(F32)
            ).astype(BF16)

        column_tiles(width, 768, one)
        go(back[j])

    hear(sends[0])
    for c, members in enumerate(IN_CHUNK):
        for j in members:
            hear(forwards[j])
        if c == 0:
            own_in.wait()
            hear(swap_in)
        first_matmul(c)
        if c < 2:
            forward(2 * c + 3)
        if c == 0:
            own_out.wait()
            hear(swap_out)
        else:
            for j in IN_CHUNK[c - 1]:
                add_and_send(j)
        second_matmul(c)
        for j in members:
            go(to_owner[j])
        if c < 2:
            forward(2 * c + 4)
        if c == 0:
            go(back_common)
            ret[block(0), :] = out[block(0), :]
    for j in IN_CHUNK[-1]:
        add_and_send(j)

    hear(back_common)
    for j in range(5):
        hear(back[j])
    partial[:, pl.ds(width, 128)] = jnp.zeros((tok_rows, 128), F32)

    def combine(first):
        rows = pl.ds(0, EARLY) if first else pl.ds(EARLY, pick.shape[0] - EARLY)

        def one(cols):
            value = lax.dot_general(
                pick[rows, :],
                ret[rows, cols],
                (((0,), (0,)), ((), ())),
                preferred_element_type=F32,
            )
            partial[:, cols] = value if first else partial[:, cols] + value

        column_tiles(width, 256, one)

    combine(True)
    for j in range(5, OWNED):
        hear(back[j])
    combine(False)

    columns = 2 * SIDE
    imgs = tok_rows // PATCH
    part = PATCH // 2

    def row_blocks(p, body):
        for i in range(imgs):

            def one(r, carry):
                off = pl.multiple_of(r * 64, 64)
                body(
                    i,
                    off,
                    pl.ds(pl.multiple_of(i * PATCH + p * part + r * 64, 64), 64),
                    pl.ds(pl.multiple_of(i * part + r * 64, 64), 64),
                )
                return carry

            lax.fori_loop(0, part // 64, one, 0)

    to_pair = []
    for p in range(2):

        def cut(i, off, rows, to):
            for c in range(columns):
                split[c % 2, c // 2, p, to, :] = partial[
                    rows, c * share : c * share + 256
                ].astype(BF16)

        row_blocks(p, cut)
        to_pair.append(
            remote(
                split.at[1 - core, :, p],
                pair.at[:, p],
                rs_send.at[p],
                rs_recv.at[p],
                other_core,
            )
        )
        go(to_pair[-1])
    over_y = []
    for p in range(2):
        hear(to_pair[p])

        def add_pair(i, off, rows, to):
            for c in range(SIDE):
                summed[c, p, to, :] = (
                    split[core, c, p, to, :].astype(F32) + pair[c, p, to, :].astype(F32)
                ).astype(BF16)

        row_blocks(p, add_pair)
        for r in (1, 3, 2):
            over_y.append(
                remote(
                    summed.at[(y + r) % SIDE, p],
                    others.at[r - 1, p],
                    rs_send.at[2 + p * 3 + r - 1],
                    rs_recv.at[2 + p * 3 + r - 1],
                    (dp, at_y(r)),
                )
            )
            go(over_y[-1])
    tail = share - 128

    def along(h, first, step):
        if (h == 0) == first:
            return (at_xz(step, 0), ex)
        return (at_xz(0, step), ex)

    gathers = []
    for p in range(2):
        for copy in over_y[3 * p : 3 * p + 3]:
            hear(copy)

        def total_up(i, off, rows, to):
            total = summed[y, p, to, :].astype(F32)
            for k in range(SIDE - 1):
                total = total + others[k, p, to, :].astype(F32)
            at = pl.ds(off, 64)
            stage_a[p][0, i, at, :] = (total[:, :128] + base[rows, 0:128]).astype(BF16)
            stage_a[p][1, i, at, 0:tail] = (
                total[:, 128:share] + base[rows, 128:share]
            ).astype(BF16)

        row_blocks(p, total_up)
        for r in (1, 3, 2):
            for h in range(2):
                k = (p * 2 + h) * 3 + r - 1
                gathers.append(
                    remote(
                        stage_a[p].at[h, pl.ds(0, imgs)],
                        stage_a[p].at[h, pl.ds(imgs * r, imgs)],
                        da_send.at[k],
                        da_recv.at[k],
                        along(h, True, r),
                    )
                )
                go(gathers[-1])

    def source_of(w, j):
        index = img[w * OWN_IMG + j]
        held = jnp.maximum(index, 0)
        device = held // imgs
        return index, device // SIDE, device % SIDE, held % imgs

    delivers = []
    for p in range(2):
        for copy in gathers[6 * p : 6 * p + 6]:
            hear(copy)
        for q in (1, 3, 2, 0):
            for h in range(2):
                w = q if h == 0 or q == 0 else SIDE - 1 + q
                for j in range(OWN_IMG):
                    _, from_x, from_z, which = source_of(w, j)
                    r = (x - from_x + SIDE) % SIDE if h == 0 else (z - from_z + SIDE) % SIDE
                    value = stage_a[p][h, r * imgs + which]
                    if q == 0:
                        stage_b[p][h, j] = value
                    else:
                        message[h, p, q - 1, j] = value
                if q:
                    k = (p * 2 + h) * 3 + q - 1
                    delivers.append(
                        remote(
                            message.at[h, p, q - 1],
                            stage_b[p].at[h, pl.ds(OWN_IMG * q, OWN_IMG)],
                            db_send.at[k],
                            db_recv.at[k],
                            along(h, False, q),
                        )
                    )
                    go(delivers[-1])
    for p in range(2):
        for copy in delivers[6 * p : 6 * p + 6]:
            hear(copy)
        for j in range(OWN_IMG):
            index, from_x, from_z, _ = source_of(0, j)
            there = index >= 0
            rows = pl.ds(j * PATCH + p * part, part)
            first = stage_b[p][0, (z - from_z + SIDE) % SIDE * OWN_IMG + j].astype(F32)
            delivered[rows, 0:128] = jnp.where(there, first, 0.0).astype(BF16)
            second = stage_b[p][1, (x - from_x + SIDE) % SIDE * OWN_IMG + j].astype(F32)
            delivered[rows, 128:share] = jnp.where(there, second, 0.0)[:, :tail].astype(BF16)
    finish()


def shards(tokens, ln_gain, ln_bias, weight_in, weight_out, expert_ids, combine_weights, owner_ids):
    groups = lax.axis_size("dp")
    columns = lax.axis_size("expert")
    tok_rows, width = tokens.shape
    share = width // columns
    hidden = 2 * weight_in.shape[2]
    experts = weight_in.shape[0] * groups

    def vmem(shape, dtype=BF16):
        return pltpu.VMEM(shape, dtype)

    def sems(count):
        return pltpu.SemaphoreType.DMA((count,))

    whole = pl.BlockSpec(memory_space=pltpu.VMEM)
    scratch = [
        pltpu.SMEM((7 * OWN_IMG,), jnp.int32),
        vmem((tok_rows, share), F32),
        vmem((tok_rows, width)),
        vmem((experts, tok_rows), F32),
        vmem((9 * CAP, tok_rows)),
        vmem((8 * CAP, width)),
        vmem((16 * CAP, width)),
        vmem((width, hidden)),
        vmem((hidden, width)),
        vmem((CHUNK, hidden)),
        vmem((16 * CAP, width)),
        vmem((OWNED * CAP, width)),
        vmem((9 * CAP, width)),
        vmem((tok_rows, width + 128), F32),
        vmem((2, SIDE, 2, tok_rows // 2, 256)),
        vmem((SIDE, 2, tok_rows // 2, 256)),
        vmem((SIDE, 2, tok_rows // 2, 256)),
        vmem((SIDE - 1, 2, tok_rows // 2, 256)),
        vmem((2, 8, PATCH // 2, 128)),
        vmem((2, 8, PATCH // 2, 128)),
        vmem((2, 2, SIDE - 1, OWN_IMG, PATCH // 2, 128)),
        vmem((2, SIDE * OWN_IMG, PATCH // 2, 128)),
        vmem((2, SIDE * OWN_IMG, PATCH // 2, 128)),
    ]
    for count in (2, 2, 2, 8, 8, 7, 7, 7, 7, 8, 8, 8, 8, 12, 12, 12, 12):
        scratch.append(sems(count))
    return pl.pallas_call(
        kernel,
        out_shape=jax.ShapeDtypeStruct((OWN_IMG * PATCH, share), BF16),
        in_specs=[pl.BlockSpec(memory_space=pltpu.SMEM)]
        + [whole] * 5
        + [pl.BlockSpec(memory_space=pl.ANY)] * 2,
        out_specs=whole,
        scratch_shapes=scratch,
        compiler_params=pltpu.CompilerParams(
            collective_id=0, has_side_effects=True, vmem_limit_bytes=67043328
        ),
    )(
        owner_ids.reshape(-1),
        tokens,
        ln_gain.reshape(-1, 128),
        ln_bias.reshape(-1, 128),
        expert_ids.T,
        combine_weights.T,
        weight_in,
        weight_out,
    ).astype(F32)


def solution(mesh):
    return jax.shard_map(
        shards,
        mesh=mesh,
        in_specs=(
            P("dp", None),
            P(),
            P(),
            P("dp", None, "expert"),
            P("dp", "expert", None),
            P("dp", None),
            P("dp", None),
            P(),
        ),
        out_specs=P("dp", "expert"),
        check_vma=False,
    )
```

time: 158 us -> 136 us (0.86)
  Pallas kernels: 148 us -> 133 us
  local copies, waits for them, and re-layouts: 7.17 us -> 2.14 us
  other arithmetic: 2.2 us -> 0 us
    pallas_call x1, Pallas kernels: 148 us -> 133 us  [shards(): pl.pallas_call(kernel, out_shape=jax.ShapeDtypeStruct((OWN_IMG * PATCH, s...]
    reshape x2 -> x0, local copies, waits for them, and re-layouts: 2.59 us -> none  [the longest x1 1.3 us: shards(): ln_bias.reshape(1, width)]
    pallas_call x1 -> x0, local copies, waits for them, and re-layouts: 2.45 us -> none  [shards(): pl.pallas_call(kernel, out_shape=jax.ShapeDtypeStruct((OWN_IMG * PATCH, s...]
    convert_element_type x0 -> x1, local copies, waits for them, and re-layouts: none -> 2.14 us  [shards(): return pl.pallas_call(kernel, out_shape=jax.ShapeDtypeStruct((OWN_IMG * P...]
    dynamic_slice x1 -> x0, local copies, waits for them, and re-layouts: 2.13 us -> none  [shards(): lax.dynamic_slice_in_dim(tokens, lax.axis_index('expert') * share, share,...]
where the time goes in v1:
time: 136 us
  Pallas kernels  133 us (98%)
  local copies, waits for them, and re-layouts  2.14 us (2%)
    pallas_call x1, Pallas kernels, shards(): pl.pallas_call(kernel, out_shape=jax.ShapeDtypeStruct((OWN_IMG * PATCH, s...  133 us

profile of v1, /device:TPU:1, one launch (start us, length us, event | category | flops | bytes accessed | tf_op | source)
XLA Modules:
  0.0 135.6 jit_solution(16128259623907813581)
XLA Ops:
  0.0 133.5 %shard_map.82 = bf16[1024,208]{1,0:T(8,128)(2,1)} custom-call(s32[32]{0:T(128)} %bitcast.9, f32[512,1664]{1,0:T(8,128)} %tokens.1, f32[13,128]{1,0:T(8,128)} %bitcast.5, f32[13,128]{1,0:T(8,128)} %bitcast.6, s32[2,512]{1,0:T(2,128)} %bitcast.7, f32[2,512]{1,0:T(2,128)} %bitcast.8, bf16[2,1664,1024]{2,1,0:T(8,128)(2,1)} %weight_in.1, ...), custom_call_target="tpu_custom_call" | custom-call | tf_op jit(solution)/shard_map/pallas_call | solution.py:599
  133.5 2.1 %copy.10 = f32[1024,208]{0,1:T(8,128)} copy(bf16[1024,208]{1,0:T(8,128)(2,1)} %shard_map.82) | data formatting | bytes 1277952 | tf_op jit(solution)/shard_map/convert_element_type | solution.py:619

commit v2 on v1

--- a/solution.py
+++ b/solution.py
@@ -15,15 +15,16 @@
 SIDE = 4
 epsilon = 1e-06
 
-COMMON = (0, 1)
-EVEN = ((2, 2), (1, 3), (3, 1), (2, 1), (3, 2), (0, 3), (1, 0))
-ODD = ((1, 1), (3, 3), (0, 2), (2, 3), (1, 2), (2, 0), (3, 0))
-OWNED = 7
-OWN_SLOT = (2, 4, 5, 8, 9, 12, 13)
-GUEST_SLOT = (3, 6, 7, 10, 11, 14, 15)
-IN_CHUNK = ((0,), (1, 2), (3, 4), (5, 6))
+NEAR = ((0, 1), (0, 3), (1, 0), (3, 0), (1, 3))
+EVEN = ((2, 2), (3, 1), (3, 3), (1, 2), (2, 1))
+ODD = ((1, 1), (0, 2), (2, 0), (2, 3), (3, 2))
+NEARS, OWNED = 5, 5
+NEAR_SLOT = (1, 2, 3, 4, 5)
+OWN_SLOT = (6, 8, 9, 12, 13)
+GUEST_SLOT = (7, 10, 11, 14, 15)
+SENT = NEARS + OWNED
 CHUNK = 4 * CAP
-EARLY = 7 * CAP
+EARLY = 9 * CAP
 
 
 def column_tiles(width, step, body):
@@ -184,7 +185,7 @@
     before = jnp.dot(named.astype(F32).astype(BF16), earlier, preferred_element_type=F32)
     rank[...] = jnp.where(named, before, 200.0)
 
-    displacements = [(0, 0), COMMON] + [owned(j) for j in range(OWNED)]
+    displacements = [(0, 0), *NEAR] + [owned(j) for j in range(OWNED)]
     place = lax.broadcasted_iota(jnp.int32, (CAP, tok_rows), 0).astype(F32)
 
     def expert_of(i):
@@ -193,7 +194,7 @@
     def hit_rows(i):
         return rank[pl.ds(expert_of(i), 1), :] == place
 
-    for i in range(2 + OWNED):
+    for i in range(1 + SENT):
         pick[block(i), :] = hit_rows(i).astype(F32).astype(BF16)
 
     pl.semaphore_wait(barrier, len(peers))
@@ -217,16 +218,15 @@
     go(swap_out)
 
     sends = []
-    for i in range(1, 2 + OWNED):
-        j = i - 2
-        slot = 1 if i == 1 else OWN_SLOT[j]
+    for i in range(SENT):
+        slot = (NEAR_SLOT + OWN_SLOT)[i]
         sends.append(
             remote(
-                gathered.at[block(i - 1), :],
+                gathered.at[block(i), :],
                 x_in.at[block(slot), :],
-                go_send.at[i - 1],
-                go_recv.at[i - 1],
-                (at_xz(*displacements[i]), ex),
+                go_send.at[i],
+                go_recv.at[i],
+                (at_xz(*displacements[i + 1]), ex),
             )
         )
 
@@ -241,10 +241,12 @@
 
         column_tiles(width, 256, one)
 
-    for start, end in ((1, 3), (3, 5), (5, 9)):
-        gather(start, end)
-        for i in range(start, end):
-            go(sends[i - 1])
+    gather(1, 4)
+    for i in range(3):
+        go(sends[i])
+    gather(4, 1 + SENT)
+    for i in (5, 3, 4, 6, 7, 8, 9):
+        go(sends[i])
 
     def own_block(cols):
         x_in[block(0), cols] = jnp.dot(
@@ -253,7 +255,7 @@
 
     column_tiles(width, 256, own_block)
 
-    for i in range(2 + OWNED):
+    for i in range(1 + SENT):
         chosen = jnp.where(ids_t[0:1, :] == expert_of(i), weights_t[0:1, :], weights_t[1:2, :])
         pick[block(i), :] = jnp.where(hit_rows(i), chosen, 0.0).astype(BF16)
 
@@ -271,41 +273,8 @@
         )
 
     def forward(j):
-        hear(sends[j + 1])
+        hear(sends[NEARS + j])
         go(forwards[j])
-
-    for j in range(3):
-        forward(j)
-
-    for c in range(2 * SIDE):
-
-        @pl.when(ex == c)
-        def _():
-            def one(r, carry):
-                rows = pl.ds(pl.multiple_of(r * 64, 64), 64)
-                base[rows, :] = tokens[rows, c * share : (c + 1) * share]
-                return carry
-
-            lax.fori_loop(0, tok_rows // 64, one, 0)
-
-    near = [dp] + [at_xz(0, q) for q in range(1, SIDE)] + [at_xz(q, 0) for q in range(1, SIDE)]
-
-    def note(i, carry):
-        owner, new = owners[i], []
-        for w, candidate in enumerate(near):
-            count, held = carry[w][0], carry[w][1:]
-            hit = owner == candidate
-            held = [jnp.where(hit & (count == k), i, held[k]) for k in range(OWN_IMG)]
-            new.append((count + hit.astype(jnp.int32), *held))
-        return tuple(new)
-
-    none = jnp.int32(-1)
-    noted = lax.fori_loop(
-        0, owners.shape[0], note, ((jnp.int32(0),) + (none,) * OWN_IMG,) * len(near)
-    )
-    for w in range(len(near)):
-        for k in range(OWN_IMG):
-            img[w * OWN_IMG + k] = noted[w][1 + k]
 
     def first_matmul(c):
         pre = jnp.dot(x_in[pl.ds(c * CHUNK, CHUNK), :], w_in[...], preferred_element_type=F32)
@@ -332,19 +301,22 @@
         back.append(
             remote(
                 out.at[block(OWN_SLOT[j]), :],
-                ret.at[block(2 + j), :],
-                rt_send.at[j],
-                rt_recv.at[j],
+                ret.at[block(1 + NEARS + j), :],
+                rt_send.at[NEARS + j],
+                rt_recv.at[NEARS + j],
                 (at_xz(-dx, -dz), ex),
             )
         )
-    back_common = remote(
-        out.at[block(1), :],
-        ret.at[block(1), :],
-        rt_send.at[OWNED],
-        rt_recv.at[OWNED],
-        (at_xz(-COMMON[0], -COMMON[1]), ex),
-    )
+    near_back = [
+        remote(
+            out.at[block(NEAR_SLOT[i]), :],
+            ret.at[block(1 + i), :],
+            rt_send.at[i],
+            rt_recv.at[i],
+            (at_xz(-dx, -dz), ex),
+        )
+        for i, (dx, dz) in enumerate(NEAR)
+    ]
 
     def add_and_send(j):
         hear(to_owner[j])
@@ -358,36 +330,78 @@
         column_tiles(width, 768, one)
         go(back[j])
 
-    hear(sends[0])
-    for c, members in enumerate(IN_CHUNK):
-        for j in members:
-            hear(forwards[j])
-        if c == 0:
-            own_in.wait()
-            hear(swap_in)
-        first_matmul(c)
-        if c < 2:
-            forward(2 * c + 3)
-        if c == 0:
-            own_out.wait()
-            hear(swap_out)
-        else:
-            for j in IN_CHUNK[c - 1]:
-                add_and_send(j)
-        second_matmul(c)
-        for j in members:
-            go(to_owner[j])
-        if c < 2:
-            forward(2 * c + 4)
-        if c == 0:
-            go(back_common)
-            ret[block(0), :] = out[block(0), :]
-    for j in IN_CHUNK[-1]:
+    for i in range(3):
+        hear(sends[i])
+    own_in.wait()
+    hear(swap_in)
+    first_matmul(0)
+    forward(0)
+    own_out.wait()
+    hear(swap_out)
+    second_matmul(0)
+    for i in range(3):
+        go(near_back[i])
+    ret[block(0), :] = out[block(0), :]
+    forward(1)
+    hear(sends[3])
+    hear(sends[4])
+    hear(forwards[0])
+    first_matmul(1)
+    forward(2)
+    second_matmul(1)
+    go(to_owner[0])
+    go(near_back[3])
+    go(near_back[4])
+    hear(forwards[1])
+    hear(forwards[2])
+    first_matmul(2)
+    forward(3)
+    forward(4)
+    add_and_send(0)
+    second_matmul(2)
+    go(to_owner[1])
+    go(to_owner[2])
+    hear(forwards[3])
+    hear(forwards[4])
+    first_matmul(3)
+    second_matmul(3)
+    go(to_owner[3])
+    go(to_owner[4])
+    for j in range(1, OWNED):
         add_and_send(j)
 
-    hear(back_common)
-    for j in range(5):
-        hear(back[j])
+    for c in range(2 * SIDE):
+
+        @pl.when(ex == c)
+        def _():
+            def one(r, carry):
+                rows = pl.ds(pl.multiple_of(r * 64, 64), 64)
+                base[rows, :] = tokens[rows, c * share : (c + 1) * share]
+                return carry
+
+            lax.fori_loop(0, tok_rows // 64, one, 0)
+
+    near = [dp] + [at_xz(0, q) for q in range(1, SIDE)] + [at_xz(q, 0) for q in range(1, SIDE)]
+
+    def note(i, carry):
+        owner, new = owners[i], []
+        for w, candidate in enumerate(near):
+            count, held = carry[w][0], carry[w][1:]
+            hit = owner == candidate
+            held = [jnp.where(hit & (count == k), i, held[k]) for k in range(OWN_IMG)]
+            new.append((count + hit.astype(jnp.int32), *held))
+        return tuple(new)
+
+    none = jnp.int32(-1)
+    noted = lax.fori_loop(
+        0, owners.shape[0], note, ((jnp.int32(0),) + (none,) * OWN_IMG,) * len(near)
+    )
+    for w in range(len(near)):
+        for k in range(OWN_IMG):
+            img[w * OWN_IMG + k] = noted[w][1 + k]
+
+    for copy in near_back + back[:3]:
+        hear(copy)
     partial[:, pl.ds(width, 128)] = jnp.zeros((tok_rows, 128), F32)
 
     def combine(first):
@@ -405,8 +419,8 @@
         column_tiles(width, 256, one)
 
     combine(True)
-    for j in range(5, OWNED):
-        hear(back[j])
+    for copy in back[3:]:
+        hear(copy)
     combine(False)
 
     columns = 2 * SIDE
@@ -574,15 +588,15 @@
         vmem((tok_rows, share), F32),
         vmem((tok_rows, width)),
         vmem((experts, tok_rows), F32),
-        vmem((9 * CAP, tok_rows)),
-        vmem((8 * CAP, width)),
+        vmem((11 * CAP, tok_rows)),
+        vmem((SENT * CAP, width)),
         vmem((16 * CAP, width)),
         vmem((width, hidden)),
         vmem((hidden, width)),
         vmem((CHUNK, hidden)),
         vmem((16 * CAP, width)),
         vmem((OWNED * CAP, width)),
-        vmem((9 * CAP, width)),
+        vmem((11 * CAP, width)),
         vmem((tok_rows, width + 128), F32),
         vmem((2, SIDE, 2, tok_rows // 2, 256)),
         vmem((SIDE, 2, tok_rows // 2, 256)),
@@ -594,7 +608,7 @@
         vmem((2, SIDE * OWN_IMG, PATCH // 2, 128)),
         vmem((2, SIDE * OWN_IMG, PATCH // 2, 128)),
     ]
-    for count in (2, 2, 2, 8, 8, 7, 7, 7, 7, 8, 8, 8, 8, 12, 12, 12, 12):
+    for count in (2, 2, 2, 10, 10, 5, 5, 5, 5, 10, 10, 8, 8, 12, 12, 12, 12):
         scratch.append(sems(count))
     return pl.pallas_call(
         kernel,

time: 136 us -> 128 us (0.941)
  Pallas kernels: 133 us -> 125 us
    pallas_call x1, Pallas kernels: 133 us -> 125 us  [shards(): pl.pallas_call(kernel, out_shape=jax.ShapeDtypeStruct((OWN_IMG * PATCH, s...]
where the time goes in v2:
time: 128 us; the launch traced here: 127 us
  Pallas kernels  125 us (98%)
  local copies, waits for them, and re-layouts  2.14 us (2%)
    pallas_call x1, Pallas kernels, shards(): pl.pallas_call(kernel, out_shape=jax.ShapeDtypeStruct((OWN_IMG * PATCH, s...  125 us

profile of v2, /device:TPU:1, one launch (start us, length us, event | category | flops | bytes accessed | tf_op | source)
XLA Modules:
  0.0 127.2 jit_solution(2320855902774288025)
XLA Ops:
  0.0 125.1 %shard_map.82 = bf16[1024,208]{1,0:T(8,128)(2,1)} custom-call(s32[32]{0:T(128)} %bitcast.9, f32[512,1664]{1,0:T(8,128)} %tokens.1, f32[13,128]{1,0:T(8,128)} %bitcast.5, f32[13,128]{1,0:T(8,128)} %bitcast.6, s32[2,512]{1,0:T(2,128)} %bitcast.7, f32[2,512]{1,0:T(2,128)} %bitcast.8, bf16[2,1664,1024]{2,1,0:T(8,128)(2,1)} %weight_in.1, ...), custom_call_target="tpu_custom_call" | custom-call | tf_op jit(solution)/shard_map/pallas_call | solution.py:613
  125.1 2.1 %copy.10 = f32[1024,208]{0,1:T(8,128)} copy(bf16[1024,208]{1,0:T(8,128)(2,1)} %shard_map.82) | data formatting | bytes 1277952 | tf_op jit(solution)/shard_map/convert_element_type | solution.py:633

commit v3 on v2

--- a/solution.py
+++ b/solution.py
@@ -175,28 +175,6 @@
 
     lax.fori_loop(0, tok_rows // 64, norm_rows, 0, unroll=2)
 
-    experts = rank.shape[0]
-    wanted = lax.broadcasted_iota(jnp.int32, (experts, tok_rows), 0)
-    named = (ids_t[0:1, :] == wanted) | (ids_t[1:2, :] == wanted)
-    earlier = (
-        lax.broadcasted_iota(jnp.int32, (tok_rows, tok_rows), 0)
-        < lax.broadcasted_iota(jnp.int32, (tok_rows, tok_rows), 1)
-    ).astype(F32).astype(BF16)
-    before = jnp.dot(named.astype(F32).astype(BF16), earlier, preferred_element_type=F32)
-    rank[...] = jnp.where(named, before, 200.0)
-
-    displacements = [(0, 0), *NEAR] + [owned(j) for j in range(OWNED)]
-    place = lax.broadcasted_iota(jnp.int32, (CAP, tok_rows), 0).astype(F32)
-
-    def expert_of(i):
-        return 2 * at_xz(*displacements[i]) + core
-
-    def hit_rows(i):
-        return rank[pl.ds(expert_of(i), 1), :] == place
-
-    for i in range(1 + SENT):
-        pick[block(i), :] = hit_rows(i).astype(F32).astype(BF16)
-
     pl.semaphore_wait(barrier, len(peers))
 
     other_core = (dp, y * 2 + 1 - core)
@@ -217,6 +195,28 @@
     go(swap_in)
     go(swap_out)
 
+    experts = rank.shape[0]
+    wanted = lax.broadcasted_iota(jnp.int32, (experts, tok_rows), 0)
+    named = (ids_t[0:1, :] == wanted) | (ids_t[1:2, :] == wanted)
+    earlier = (
+        lax.broadcasted_iota(jnp.int32, (tok_rows, tok_rows), 0)
+        < lax.broadcasted_iota(jnp.int32, (tok_rows, tok_rows), 1)
+    ).astype(F32).astype(BF16)
+    before = jnp.dot(named.astype(F32).astype(BF16), earlier, preferred_element_type=F32)
+    rank[...] = jnp.where(named, before, 200.0)
+
+    displacements = [(0, 0), *NEAR] + [owned(j) for j in range(OWNED)]
+    place = lax.broadcasted_iota(jnp.int32, (CAP, tok_rows), 0).astype(F32)
+
+    def expert_of(i):
+        return 2 * at_xz(*displacements[i]) + core
+
+    def hit_rows(i):
+        return rank[pl.ds(expert_of(i), 1), :] == place
+
+    for i in range(1 + SENT):
+        pick[block(i), :] = hit_rows(i).astype(F32).astype(BF16)
+
     sends = []
     for i in range(SENT):
         slot = (NEAR_SLOT + OWN_SLOT)[i]
@@ -241,12 +241,10 @@
 
         column_tiles(width, 256, one)
 
-    gather(1, 4)
-    for i in range(3):
-        go(sends[i])
-    gather(4, 1 + SENT)
-    for i in (5, 3, 4, 6, 7, 8, 9):
-        go(sends[i])
+    for start, end in ((6, 7), (1, 4), (7, 8), (4, 6), (8, 1 + SENT)):
+        gather(start, end)
+        for i in range(start, end):
+            go(sends[i - 1])
 
     def own_block(cols):
         x_in[block(0), cols] = jnp.dot(
@@ -330,19 +328,19 @@
         column_tiles(width, 768, one)
         go(back[j])
 
+    forward(0)
     for i in range(3):
         hear(sends[i])
     own_in.wait()
     hear(swap_in)
     first_matmul(0)
-    forward(0)
+    forward(1)
     own_out.wait()
     hear(swap_out)
     second_matmul(0)
     for i in range(3):
         go(near_back[i])
     ret[block(0), :] = out[block(0), :]
-    forward(1)
     hear(sends[3])
     hear(sends[4])
     hear(forwards[0])
@@ -352,10 +350,10 @@
     go(to_owner[0])
     go(near_back[3])
     go(near_back[4])
+    forward(3)
     hear(forwards[1])
     hear(forwards[2])
     first_matmul(2)
-    forward(3)
     forward(4)
     add_and_send(0)
     second_matmul(2)
@@ -364,11 +362,13 @@
     hear(forwards[3])
     hear(forwards[4])
     first_matmul(3)
+    add_and_send(1)
+    add_and_send(2)
     second_matmul(3)
     go(to_owner[3])
     go(to_owner[4])
-    for j in range(1, OWNED):
-        add_and_send(j)
+    add_and_send(3)
+    add_and_send(4)
 
     for c in range(2 * SIDE):
 
@@ -473,7 +473,7 @@
                 ).astype(BF16)
 
         row_blocks(p, add_pair)
-        for r in (1, 3, 2):
+        for r in (2, 1, 3):
             over_y.append(
                 remote(
                     summed.at[(y + r) % SIDE, p],
@@ -507,7 +507,7 @@
             ).astype(BF16)
 
         row_blocks(p, total_up)
-        for r in (1, 3, 2):
+        for r in (2, 1, 3):
             for h in range(2):
                 k = (p * 2 + h) * 3 + r - 1
                 gathers.append(
@@ -531,7 +531,7 @@
     for p in range(2):
         for copy in gathers[6 * p : 6 * p + 6]:
             hear(copy)
-        for q in (1, 3, 2, 0):
+        for q in (2, 1, 3, 0):
             for h in range(2):
                 w = q if h == 0 or q == 0 else SIDE - 1 + q
                 for j in range(OWN_IMG):

time: 128 us -> 138 us (1.078)
  Pallas kernels: 125 us -> 134 us
    pallas_call x1, Pallas kernels: 125 us -> 134 us  [shards(): pl.pallas_call(kernel, out_shape=jax.ShapeDtypeStruct((OWN_IMG * PATCH, s...]
where the time goes in v3:
time: 138 us; the launch traced here: 136 us
  Pallas kernels  134 us (97%)
  local copies, waits for them, and re-layouts  2.14 us (2%)
    pallas_call x1, Pallas kernels, shards(): pl.pallas_call(kernel, out_shape=jax.ShapeDtypeStruct((OWN_IMG * PATCH, s...  134 us

profile of v3, /device:TPU:1, one launch (start us, length us, event | category | flops | bytes accessed | tf_op | source)
XLA Modules:
  0.0 136.2 jit_solution(14119707761880066656)
XLA Ops:
  0.0 134.1 %shard_map.82 = bf16[1024,208]{1,0:T(8,128)(2,1)} custom-call(s32[32]{0:T(128)} %bitcast.9, f32[512,1664]{1,0:T(8,128)} %tokens.1, f32[13,128]{1,0:T(8,128)} %bitcast.5, f32[13,128]{1,0:T(8,128)} %bitcast.6, s32[2,512]{1,0:T(2,128)} %bitcast.7, f32[2,512]{1,0:T(2,128)} %bitcast.8, bf16[2,1664,1024]{2,1,0:T(8,128)(2,1)} %weight_in.1, ...), custom_call_target="tpu_custom_call" | custom-call | tf_op jit(solution)/shard_map/pallas_call | solution.py:613
  134.1 2.1 %copy.10 = f32[1024,208]{0,1:T(8,128)} copy(bf16[1024,208]{1,0:T(8,128)(2,1)} %shard_map.82) | data formatting | bytes 1277952 | tf_op jit(solution)/shard_map/convert_element_type | solution.py:633
